TPU v7x, 512 devices: a whole 4x4x16 slice. The times are simulated.
512 devices in a mesh: gx: 64 (over z, x_hi, core), gy: 8 (over x_lo, y).
Axes of the slice: x: 4 (x_hi: 2, x_lo: 2; x = x_hi * 2 + x_lo), y: 4, z: 16, core: 2. Of those that a mesh axis runs over, the one named last changes fastest.
Arguments:
- initial: float32 [256, 1024, 512], P('gx', 'gy'), may hold values from -4 to 4
- kappa: float32 [256, 1024, 512], P('gx', 'gy'), may hold values from 0.04 to 0.12
- velocity: float32 [256, 1024, 512], P('gx', 'gy'), may hold values from 0.05 to 0.2
- rate: float32 [256, 1024, 512], P('gx', 'gy'), may hold values from 0.05 to 0.3
Outputs:
- final: float32 [256, 1024, 512], P('gx', 'gy')
All inputs are finite; a program needn't handle non-finite values.
Results may differ from a plain program's by a relative error of at most 0.00002.
Values sent between devices are 32-bit elements; how exact they have to be, the bound alone decides.
A program may use at most 64 MiB of HBM per device.

v0:
```python
import jax
import jax.numpy as jnp
from jax import lax
from jax.sharding import PartitionSpec as P

STEPS = 4
ITERS = 2


robin_p = 0.6


def extended(cells, sides, width):
    for axis, dim in sides:
        count = lax.axis_size(axis)
        ends = count - 1
        head = lax.slice_in_dim(cells, 0, width, axis=dim)
        tail = lax.slice_in_dim(cells, cells.shape[dim] - width, cells.shape[dim], axis=dim)
        cells = jnp.concatenate(
            [
                lax.ppermute(tail, axis, [(i, (i + 1) % count) for i in range(ends)]),
                cells,
                lax.ppermute(head, axis, [((i + 1) % count, i) for i in range(ends)]),
            ],
            axis=dim,
        )
    return cells


def passed_along(value, axis, steps):
    count = lax.axis_size(axis)
    pairs = [(source, (source + steps) % count) for source in range(count)]
    return lax.ppermute(value, axis, pairs)


def make_ghosts(field, data_left, data_right):
    first = field[0]
    last = field[-1]
    ghost_left = (data_left + first * (1.0 - robin_p / 2)) / (1.0 + robin_p / 2)
    ghost_right = (data_right + last * (1.0 - robin_p / 2)) / (1.0 + robin_p / 2)
    return (first, ghost_left, last, ghost_right)


def stencil(center, minus_x, plus_x, upper, lower, kappa, velocity, rate):
    plus_z = jnp.pad(center[:, :, 1:], ((0, 0), (0, 0), (0, 1)))
    minus_z = jnp.pad(center[:, :, :-1], ((0, 0), (0, 0), (1, 0)))
    lap = plus_x + minus_x
    lap = lap + upper + lower
    lap = lap + plus_z + minus_z
    lap = lap - 6.0 * center
    react = rate * center**3 / (1.0 + center * center)
    return center + kappa * lap - velocity * (center - minus_x) - react


def advance(field, kappa, velocity, rate, data_left, data_right):
    first, ghost_left, last, ghost_right = make_ghosts(field, data_left, data_right)
    widened = extended(field, (("gy", 1),), 1)
    minus_x = jnp.concatenate([ghost_left[None], field[:-1]], axis=0)
    plus_x = jnp.concatenate([field[1:], ghost_right[None]], axis=0)
    updated = stencil(
        field, minus_x, plus_x, widened[:, 2:], widened[:, :-2], kappa, velocity, rate
    )
    return (updated, first, ghost_left, last, ghost_right)


def combine_data(value, ghost):
    return value - ghost + robin_p * (value + ghost) / 2


def local(initial, kappa, velocity, rate):
    rows_own = initial.shape[1]
    start, kappa_w, velocity_w, rate_w = (initial, kappa, velocity, rate)
    margin = 0
    full_rows = rows_own + 2 * margin
    zero_plane = jnp.zeros((full_rows, initial.shape[2]), jnp.float32)
    data_left = jnp.stack([zero_plane] * STEPS)
    data_right = jnp.stack([zero_plane] * STEPS)
    field = start
    for sweep in range(ITERS):
        field = start
        firsts, lefts, lasts, rights = ([], [], [], [])
        for step in range(STEPS):
            field, first, ghost_left, last, ghost_right = advance(
                field, kappa_w, velocity_w, rate_w, data_left[step], data_right[step]
            )
            firsts.append(first)
            lefts.append(ghost_left)
            lasts.append(last)
            rights.append(ghost_right)
        if sweep + 1 < ITERS:
            backward = jnp.stack([jnp.stack(firsts), jnp.stack(lefts)])
            forward = jnp.stack([jnp.stack(lasts), jnp.stack(rights)])
            got_next = passed_along(backward, "gx", -1)
            got_prev = passed_along(forward, "gx", 1)
            data_right = combine_data(got_next[0], got_next[1])
            data_left = combine_data(got_prev[0], got_prev[1])
    return field


def solution(mesh):
    placed = (P("gx", "gy", None), P("gx", "gy", None), P("gx", "gy", None), P("gx", "gy", None))
    return jax.shard_map(
        local, mesh=mesh, in_specs=placed, out_specs=P("gx", "gy", None), check_vma=False
    )
```

profile of v0, /device:TPU:230, one launch (start us, length us, event | category | flops | bytes accessed | tf_op | source)
XLA Modules:
  0.0 128.5 jit_solution(7037590987735334436)
XLA Ops:
  1.0 5.2 %collective-permute-start = (f32[4,1,512]{2,1,0:T(1,128)S(1)}, f32[4,1,512]{2,1,0:T(1,128)S(1)}, u32[]{:S(2)}, u32[]{:S(2)}) collective-permute-start(f32[4,1,512]{2,1,0:T(1,128)S(1)} %get-tuple-element.63), channel_id=1, source_target_pairs={{1,0},{2,1},{3,2},{4,3},{5,4},{6,5},{7,6},{9,8},{10,9},{11,10},{12... | collective-permute-start | bytes 24584 | tf_op jit(solution)/shard_map/ppermute | solution.py:23
  6.2 1.9 %collective-permute-start.1 = (f32[4,1,512]{2,1,0:T(1,128)S(1)}, f32[4,1,512]{2,1,0:T(1,128)S(1)}, u32[]{:S(2)}, u32[]{:S(2)}) collective-permute-start(f32[4,1,512]{2,1,0:T(1,128)S(1)} %get-tuple-element.64), channel_id=1, source_target_pairs={{0,1},{1,2},{2,3},{3,4},{4,5},{5,6},{6,7},{8,9},{9,10},{10,11},{11... | collective-permute-start | bytes 24584 | tf_op jit(solution)/shard_map/ppermute | solution.py:21
  8.1 1.5 %fusion.116 = (f32[3,128,512]{2,1,0:T(8,128)S(1)}, f32[3,128,512]{2,1,0:T(8,128)S(1)}) fusion(f32[4,128,512]{2,1,0:T(8,128)} %param.4), kind=kLoop, calls=%fused_computation.184 | loop fusion | bytes 3145728 | tf_op jit(solution)/shard_map/slice | solution.py:58
  10.2 3.7 %collective-permute-done.1 = f32[4,1,512]{2,1,0:T(1,128)S(1)} collective-permute-done((f32[4,1,512]{2,1,0:T(1,128)S(1)}, f32[4,1,512]{2,1,0:T(1,128)S(1)}, u32[]{:S(2)}, u32[]{:S(2)}) %collective-permute-start.1) | collective-permute-done | bytes 8224 | tf_op jit(solution)/shard_map/ppermute | solution.py:21
  15.6 3.7 %collective-permute-start.2 = (f32[4,1,512]{2,1,0:T(1,128)S(1)}, f32[4,1,512]{2,1,0:T(1,128)S(1)}, u32[]{:S(2)}, u32[]{:S(2)}) collective-permute-start(f32[4,1,512]{2,1,0:T(1,128)S(1)} %get-tuple-element.57), channel_id=1, source_target_pairs={{1,0},{2,1},{3,2},{4,3},{5,4},{6,5},{7,6},{9,8},{10,9},{11,10},{12... | collective-permute-start | bytes 24584 | tf_op jit(solution)/shard_map/ppermute | solution.py:23
  19.2 2.2 %collective-permute-start.3 = (f32[4,1,512]{2,1,0:T(1,128)S(1)}, f32[4,1,512]{2,1,0:T(1,128)S(1)}, u32[]{:S(2)}, u32[]{:S(2)}) collective-permute-start(f32[4,1,512]{2,1,0:T(1,128)S(1)} %get-tuple-element.58), channel_id=1, source_target_pairs={{0,1},{1,2},{2,3},{3,4},{4,5},{5,6},{6,7},{8,9},{9,10},{10,11},{11... | collective-permute-start | bytes 24584 | tf_op jit(solution)/shard_map/ppermute | solution.py:21
  21.6 5.3 %collective-permute-done.3 = f32[4,1,512]{2,1,0:T(1,128)S(1)} collective-permute-done((f32[4,1,512]{2,1,0:T(1,128)S(1)}, f32[4,1,512]{2,1,0:T(1,128)S(1)}, u32[]{:S(2)}, u32[]{:S(2)}) %collective-permute-start.3) | collective-permute-done | bytes 8224 | tf_op jit(solution)/shard_map/ppermute | solution.py:21
  28.6 1.9 %collective-permute-start.4 = (f32[4,1,512]{2,1,0:T(1,128)S(1)}, f32[4,1,512]{2,1,0:T(1,128)S(1)}, u32[]{:S(2)}, u32[]{:S(2)}) collective-permute-start(f32[4,1,512]{2,1,0:T(1,128)S(1)} %get-tuple-element.51), channel_id=1, source_target_pairs={{1,0},{2,1},{3,2},{4,3},{5,4},{6,5},{7,6},{9,8},{10,9},{11,10},{12... | collective-permute-start | bytes 24584 | tf_op jit(solution)/shard_map/ppermute | solution.py:23
  30.6 3.9 %collective-permute-start.5 = (f32[4,1,512]{2,1,0:T(1,128)S(1)}, f32[4,1,512]{2,1,0:T(1,128)S(1)}, u32[]{:S(2)}, u32[]{:S(2)}) collective-permute-start(f32[4,1,512]{2,1,0:T(1,128)S(1)} %get-tuple-element.52), channel_id=1, source_target_pairs={{0,1},{1,2},{2,3},{3,4},{4,5},{5,6},{6,7},{8,9},{9,10},{10,11},{11... | collective-permute-start | bytes 24584 | tf_op jit(solution)/shard_map/ppermute | solution.py:21
  34.6 3.6 %collective-permute-done.5 = f32[4,1,512]{2,1,0:T(1,128)S(1)} collective-permute-done((f32[4,1,512]{2,1,0:T(1,128)S(1)}, f32[4,1,512]{2,1,0:T(1,128)S(1)}, u32[]{:S(2)}, u32[]{:S(2)}) %collective-permute-start.5) | collective-permute-done | bytes 8224 | tf_op jit(solution)/shard_map/ppermute | solution.py:21
  39.9 1.9 %collective-permute-start.6 = (f32[2,4,128,512]{3,2,1,0:T(8,128)S(1)}, f32[2,4,128,512]{3,2,1,0:T(8,128)S(1)}, u32[]{:S(2)}, u32[]{:S(2)}) collective-permute-start(f32[2,4,128,512]{3,2,1,0:T(8,128)S(1)} %pad_maximum_fusion), channel_id=1, source_target_pairs={{0,504},{8,0},{16,8},{24,16},{32,24},{40,32},{48,40},{56,48},{64,5... | collective-permute-start | bytes 6291464 | tf_op jit(solution)/shard_map/ppermute | solution.py:33
  42.2 2.4 %collective-permute-start.7 = (f32[2,4,128,512]{3,2,1,0:T(8,128)S(1)}, f32[2,4,128,512]{3,2,1,0:T(8,128)S(1)}, u32[]{:S(2)}, u32[]{:S(2)}) collective-permute-start(f32[2,4,128,512]{3,2,1,0:T(8,128)S(1)} %pad_maximum_fusion.1), channel_id=1, source_target_pairs={{0,8},{8,16},{16,24},{24,32},{32,40},{40,48},{48,56},{56,64},{64,7... | collective-permute-start | bytes 6291464 | tf_op jit(solution)/shard_map/ppermute | solution.py:33
  44.6 43.3 %collective-permute-done.6 = f32[2,4,128,512]{3,2,1,0:T(8,128)S(1)} collective-permute-done((f32[2,4,128,512]{3,2,1,0:T(8,128)S(1)}, f32[2,4,128,512]{3,2,1,0:T(8,128)S(1)}, u32[]{:S(2)}, u32[]{:S(2)}) %collective-permute-start.6) | collective-permute-done | bytes 2097184 | tf_op jit(solution)/shard_map/ppermute | solution.py:33
  88.2 3.9 %collective-permute-done.7 = f32[2,4,128,512]{3,2,1,0:T(8,128)S(1)} collective-permute-done((f32[2,4,128,512]{3,2,1,0:T(8,128)S(1)}, f32[2,4,128,512]{3,2,1,0:T(8,128)S(1)}, u32[]{:S(2)}, u32[]{:S(2)}) %collective-permute-start.7) | collective-permute-done | bytes 2097184 | tf_op jit(solution)/shard_map/ppermute | solution.py:33
  94.2 1.9 %collective-permute-start.8 = (f32[4,1,512]{2,1,0:T(1,128)S(1)}, f32[4,1,512]{2,1,0:T(1,128)S(1)}, u32[]{:S(2)}, u32[]{:S(2)}) collective-permute-start(f32[4,1,512]{2,1,0:T(1,128)S(1)} %get-tuple-element.27), channel_id=1, source_target_pairs={{1,0},{2,1},{3,2},{4,3},{5,4},{6,5},{7,6},{9,8},{10,9},{11,10},{12... | collective-permute-start | bytes 24584 | tf_op jit(solution)/shard_map/ppermute | solution.py:23
  96.1 3.9 %collective-permute-start.9 = (f32[4,1,512]{2,1,0:T(1,128)S(1)}, f32[4,1,512]{2,1,0:T(1,128)S(1)}, u32[]{:S(2)}, u32[]{:S(2)}) collective-permute-start(f32[4,1,512]{2,1,0:T(1,128)S(1)} %get-tuple-element.28), channel_id=1, source_target_pairs={{0,1},{1,2},{2,3},{3,4},{4,5},{5,6},{6,7},{8,9},{9,10},{10,11},{11... | collective-permute-start | bytes 24584 | tf_op jit(solution)/shard_map/ppermute | solution.py:21
  100.2 3.6 %collective-permute-done.9 = f32[4,1,512]{2,1,0:T(1,128)S(1)} collective-permute-done((f32[4,1,512]{2,1,0:T(1,128)S(1)}, f32[4,1,512]{2,1,0:T(1,128)S(1)}, u32[]{:S(2)}, u32[]{:S(2)}) %collective-permute-start.9) | collective-permute-done | bytes 8224 | tf_op jit(solution)/shard_map/ppermute | solution.py:21
  105.5 1.9 %collective-permute-start.10 = (f32[4,1,512]{2,1,0:T(1,128)S(1)}, f32[4,1,512]{2,1,0:T(1,128)S(1)}, u32[]{:S(2)}, u32[]{:S(2)}) collective-permute-start(f32[4,1,512]{2,1,0:T(1,128)S(1)} %get-tuple-element.19), channel_id=1, source_target_pairs={{1,0},{2,1},{3,2},{4,3},{5,4},{6,5},{7,6},{9,8},{10,9},{11,10},{12... | collective-permute-start | bytes 24584 | tf_op jit(solution)/shard_map/ppermute | solution.py:23
  107.4 4.1 %collective-permute-start.11 = (f32[4,1,512]{2,1,0:T(1,128)S(1)}, f32[4,1,512]{2,1,0:T(1,128)S(1)}, u32[]{:S(2)}, u32[]{:S(2)}) collective-permute-start(f32[4,1,512]{2,1,0:T(1,128)S(1)} %get-tuple-element.20), channel_id=1, source_target_pairs={{0,1},{1,2},{2,3},{3,4},{4,5},{5,6},{6,7},{8,9},{9,10},{10,11},{11... | collective-permute-start | bytes 24584 | tf_op jit(solution)/shard_map/ppermute | solution.py:21
  111.7 3.4 %collective-permute-done.11 = f32[4,1,512]{2,1,0:T(1,128)S(1)} collective-permute-done((f32[4,1,512]{2,1,0:T(1,128)S(1)}, f32[4,1,512]{2,1,0:T(1,128)S(1)}, u32[]{:S(2)}, u32[]{:S(2)}) %collective-permute-start.11) | collective-permute-done | bytes 8224 | tf_op jit(solution)/shard_map/ppermute | solution.py:21
  116.8 1.9 %collective-permute-start.12 = (f32[4,1,512]{2,1,0:T(1,128)S(1)}, f32[4,1,512]{2,1,0:T(1,128)S(1)}, u32[]{:S(2)}, u32[]{:S(2)}) collective-permute-start(f32[4,1,512]{2,1,0:T(1,128)S(1)} %get-tuple-element.11), channel_id=1, source_target_pairs={{1,0},{2,1},{3,2},{4,3},{5,4},{6,5},{7,6},{9,8},{10,9},{11,10},{12... | collective-permute-start | bytes 24584 | tf_op jit(solution)/shard_map/ppermute | solution.py:23
  118.8 3.9 %collective-permute-start.13 = (f32[4,1,512]{2,1,0:T(1,128)S(1)}, f32[4,1,512]{2,1,0:T(1,128)S(1)}, u32[]{:S(2)}, u32[]{:S(2)}) collective-permute-start(f32[4,1,512]{2,1,0:T(1,128)S(1)} %get-tuple-element.12), channel_id=1, source_target_pairs={{0,1},{1,2},{2,3},{3,4},{4,5},{5,6},{6,7},{8,9},{9,10},{10,11},{11... | collective-permute-start | bytes 24584 | tf_op jit(solution)/shard_map/ppermute | solution.py:21
  122.8 3.6 %collective-permute-done.13 = f32[4,1,512]{2,1,0:T(1,128)S(1)} collective-permute-done((f32[4,1,512]{2,1,0:T(1,128)S(1)}, f32[4,1,512]{2,1,0:T(1,128)S(1)}, u32[]{:S(2)}, u32[]{:S(2)}) %collective-permute-start.13) | collective-permute-done | bytes 8224 | tf_op jit(solution)/shard_map/ppermute | solution.py:21
  126.4 2.1 %fusion.39 = f32[4,128,512]{2,1,0:T(8,128)} fusion(f32[4,128,512]{2,1,0:T(8,128)S(1)} %copy-done, f32[4,128,512]{2,1,0:T(8,128)S(1)} %fusion.36, f32[4,128,512]{2,1,0:T(8,128)S(1)} %copy-done.1, f32[4,1,512]{2,1,0:T(1,128)S(1)} %collective-permute-done.13, f32[4,1,512]{2,1,0:T(1,128)S(1)} %collective-permute-done.12, ...), kind=kLoop, calls=%fused_computation.58 | loop fusion | flops 5767168 | bytes 9449472 | tf_op jit(solution)/shard_map/sub | solution.py:52
  (51 shorter events, 13.3 us)
Async XLA Ops:
  0.0 9.6 %copy-start.3 = (f32[4,128,512]{2,1,0:T(8,128)S(1)}, f32[4,128,512]{2,1,0:T(8,128)}, u32[]{:S(2)}) copy-start(f32[4,128,512]{2,1,0:T(8,128)} %param.4) | copy-start | bytes 3145732
  1.0 9.2 %collective-permute-start = (f32[4,1,512]{2,1,0:T(1,128)S(1)}, f32[4,1,512]{2,1,0:T(1,128)S(1)}, u32[]{:S(2)}, u32[]{:S(2)}) collective-permute-start(f32[4,1,512]{2,1,0:T(1,128)S(1)} %get-tuple-element.63), channel_id=1, source_target_pairs={{1,0},{2,1},{3,2},{4,3},{5,4},{6,5},{7,6},{9,8},{10,9},{11,10},{12... | collective-permute-start | bytes 24584 | tf_op jit(solution)/shard_map/ppermute | solution.py:23
  6.2 7.7 %collective-permute-start.1 = (f32[4,1,512]{2,1,0:T(1,128)S(1)}, f32[4,1,512]{2,1,0:T(1,128)S(1)}, u32[]{:S(2)}, u32[]{:S(2)}) collective-permute-start(f32[4,1,512]{2,1,0:T(1,128)S(1)} %get-tuple-element.64), channel_id=1, source_target_pairs={{0,1},{1,2},{2,3},{3,4},{4,5},{5,6},{6,7},{8,9},{9,10},{10,11},{11... | collective-permute-start | bytes 24584 | tf_op jit(solution)/shard_map/ppermute | solution.py:21
  9.6 4.2 %copy-start = (f32[4,128,512]{2,1,0:T(8,128)S(1)}, f32[4,128,512]{2,1,0:T(8,128)}, u32[]{:S(2)}) copy-start(f32[4,128,512]{2,1,0:T(8,128)} %param.7) | copy-start | bytes 3145732
  9.6 4.2 %copy-start.1 = (f32[4,128,512]{2,1,0:T(8,128)S(1)}, f32[4,128,512]{2,1,0:T(8,128)}, u32[]{:S(2)}) copy-start(f32[4,128,512]{2,1,0:T(8,128)} %param.5) | copy-start | bytes 3145732
  9.6 4.2 %copy-start.2 = (f32[4,128,512]{2,1,0:T(8,128)S(1)}, f32[4,128,512]{2,1,0:T(8,128)}, u32[]{:S(2)}) copy-start(f32[4,128,512]{2,1,0:T(8,128)} %param.6) | copy-start | bytes 3145732
  15.6 6.0 %collective-permute-start.2 = (f32[4,1,512]{2,1,0:T(1,128)S(1)}, f32[4,1,512]{2,1,0:T(1,128)S(1)}, u32[]{:S(2)}, u32[]{:S(2)}) collective-permute-start(f32[4,1,512]{2,1,0:T(1,128)S(1)} %get-tuple-element.57), channel_id=1, source_target_pairs={{1,0},{2,1},{3,2},{4,3},{5,4},{6,5},{7,6},{9,8},{10,9},{11,10},{12... | collective-permute-start | bytes 24584 | tf_op jit(solution)/shard_map/ppermute | solution.py:23
  19.2 7.7 %collective-permute-start.3 = (f32[4,1,512]{2,1,0:T(1,128)S(1)}, f32[4,1,512]{2,1,0:T(1,128)S(1)}, u32[]{:S(2)}, u32[]{:S(2)}) collective-permute-start(f32[4,1,512]{2,1,0:T(1,128)S(1)} %get-tuple-element.58), channel_id=1, source_target_pairs={{0,1},{1,2},{2,3},{3,4},{4,5},{5,6},{6,7},{8,9},{9,10},{10,11},{11... | collective-permute-start | bytes 24584 | tf_op jit(solution)/shard_map/ppermute | solution.py:21
  28.6 6.0 %collective-permute-start.4 = (f32[4,1,512]{2,1,0:T(1,128)S(1)}, f32[4,1,512]{2,1,0:T(1,128)S(1)}, u32[]{:S(2)}, u32[]{:S(2)}) collective-permute-start(f32[4,1,512]{2,1,0:T(1,128)S(1)} %get-tuple-element.51), channel_id=1, source_target_pairs={{1,0},{2,1},{3,2},{4,3},{5,4},{6,5},{7,6},{9,8},{10,9},{11,10},{12... | collective-permute-start | bytes 24584 | tf_op jit(solution)/shard_map/ppermute | solution.py:23
  30.6 7.7 %collective-permute-start.5 = (f32[4,1,512]{2,1,0:T(1,128)S(1)}, f32[4,1,512]{2,1,0:T(1,128)S(1)}, u32[]{:S(2)}, u32[]{:S(2)}) collective-permute-start(f32[4,1,512]{2,1,0:T(1,128)S(1)} %get-tuple-element.52), channel_id=1, source_target_pairs={{0,1},{1,2},{2,3},{3,4},{4,5},{5,6},{6,7},{8,9},{9,10},{10,11},{11... | collective-permute-start | bytes 24584 | tf_op jit(solution)/shard_map/ppermute | solution.py:21
  39.9 48.1 %collective-permute-start.6 = (f32[2,4,128,512]{3,2,1,0:T(8,128)S(1)}, f32[2,4,128,512]{3,2,1,0:T(8,128)S(1)}, u32[]{:S(2)}, u32[]{:S(2)}) collective-permute-start(f32[2,4,128,512]{3,2,1,0:T(8,128)S(1)} %pad_maximum_fusion), channel_id=1, source_target_pairs={{0,504},{8,0},{16,8},{24,16},{32,24},{40,32},{48,40},{56,48},{64,5... | collective-permute-start | bytes 6291464 | tf_op jit(solution)/shard_map/ppermute | solution.py:33
  42.2 49.9 %collective-permute-start.7 = (f32[2,4,128,512]{3,2,1,0:T(8,128)S(1)}, f32[2,4,128,512]{3,2,1,0:T(8,128)S(1)}, u32[]{:S(2)}, u32[]{:S(2)}) collective-permute-start(f32[2,4,128,512]{3,2,1,0:T(8,128)S(1)} %pad_maximum_fusion.1), channel_id=1, source_target_pairs={{0,8},{8,16},{16,24},{24,32},{32,40},{40,48},{48,56},{56,64},{64,7... | collective-permute-start | bytes 6291464 | tf_op jit(solution)/shard_map/ppermute | solution.py:33
  94.2 6.0 %collective-permute-start.8 = (f32[4,1,512]{2,1,0:T(1,128)S(1)}, f32[4,1,512]{2,1,0:T(1,128)S(1)}, u32[]{:S(2)}, u32[]{:S(2)}) collective-permute-start(f32[4,1,512]{2,1,0:T(1,128)S(1)} %get-tuple-element.27), channel_id=1, source_target_pairs={{1,0},{2,1},{3,2},{4,3},{5,4},{6,5},{7,6},{9,8},{10,9},{11,10},{12... | collective-permute-start | bytes 24584 | tf_op jit(solution)/shard_map/ppermute | solution.py:23
  96.1 7.7 %collective-permute-start.9 = (f32[4,1,512]{2,1,0:T(1,128)S(1)}, f32[4,1,512]{2,1,0:T(1,128)S(1)}, u32[]{:S(2)}, u32[]{:S(2)}) collective-permute-start(f32[4,1,512]{2,1,0:T(1,128)S(1)} %get-tuple-element.28), channel_id=1, source_target_pairs={{0,1},{1,2},{2,3},{3,4},{4,5},{5,6},{6,7},{8,9},{9,10},{10,11},{11... | collective-permute-start | bytes 24584 | tf_op jit(solution)/shard_map/ppermute | solution.py:21
  105.5 6.2 %collective-permute-start.10 = (f32[4,1,512]{2,1,0:T(1,128)S(1)}, f32[4,1,512]{2,1,0:T(1,128)S(1)}, u32[]{:S(2)}, u32[]{:S(2)}) collective-permute-start(f32[4,1,512]{2,1,0:T(1,128)S(1)} %get-tuple-element.19), channel_id=1, source_target_pairs={{1,0},{2,1},{3,2},{4,3},{5,4},{6,5},{7,6},{9,8},{10,9},{11,10},{12... | collective-permute-start | bytes 24584 | tf_op jit(solution)/shard_map/ppermute | solution.py:23
  107.4 7.7 %collective-permute-start.11 = (f32[4,1,512]{2,1,0:T(1,128)S(1)}, f32[4,1,512]{2,1,0:T(1,128)S(1)}, u32[]{:S(2)}, u32[]{:S(2)}) collective-permute-start(f32[4,1,512]{2,1,0:T(1,128)S(1)} %get-tuple-element.20), channel_id=1, source_target_pairs={{0,1},{1,2},{2,3},{3,4},{4,5},{5,6},{6,7},{8,9},{9,10},{10,11},{11... | collective-permute-start | bytes 24584 | tf_op jit(solution)/shard_map/ppermute | solution.py:21
  116.8 6.0 %collective-permute-start.12 = (f32[4,1,512]{2,1,0:T(1,128)S(1)}, f32[4,1,512]{2,1,0:T(1,128)S(1)}, u32[]{:S(2)}, u32[]{:S(2)}) collective-permute-start(f32[4,1,512]{2,1,0:T(1,128)S(1)} %get-tuple-element.11), channel_id=1, source_target_pairs={{1,0},{2,1},{3,2},{4,3},{5,4},{6,5},{7,6},{9,8},{10,9},{11,10},{12... | collective-permute-start | bytes 24584 | tf_op jit(solution)/shard_map/ppermute | solution.py:23
  118.8 7.7 %collective-permute-start.13 = (f32[4,1,512]{2,1,0:T(1,128)S(1)}, f32[4,1,512]{2,1,0:T(1,128)S(1)}, u32[]{:S(2)}, u32[]{:S(2)}) collective-permute-start(f32[4,1,512]{2,1,0:T(1,128)S(1)} %get-tuple-element.12), channel_id=1, source_target_pairs={{0,1},{1,2},{2,3},{3,4},{4,5},{5,6},{6,7},{8,9},{9,10},{10,11},{11... | collective-permute-start | bytes 24584 | tf_op jit(solution)/shard_map/ppermute | solution.py:21
where the time goes:
time: 129 us; the launch traced here: 128 us
  waiting for transfers between devices  70.4 us (55%)
  starting transfers between devices  40.8 us (32%)
  other arithmetic  11 us (9%)
  local copies, waits for them, and re-layouts  5.83 us (5%)
    ppermute x2, waiting for transfers between devices, passed_along(): return lax.ppermute(value, axis, pairs)  47.2 us
    ppermute x6, waiting for transfers between devices, extended(): lax.ppermute(tail, axis, [(i, (i + 1) % count) for i in range(ends)])  23.2 us
    ppermute x6, starting transfers between devices, extended(): lax.ppermute(tail, axis, [(i, (i + 1) % count) for i in range(ends)])  20 us
    ppermute x6, starting transfers between devices, extended(): lax.ppermute(head, axis, [((i + 1) % count, i) for i in range(ends)])  16.5 us
    sub x7, other arithmetic, stencil(): return center + kappa * lap - velocity * (center - minus_x) - react  8.74 us
    ppermute x2, starting transfers between devices, passed_along(): return lax.ppermute(value, axis, pairs)  4.33 us
  transfers between devices with their start and end apart: 14, of which 8 were waited for; matrix products, arithmetic and copies ran while one was open for 3% of the time, Pallas kernels for 0%

commit v1 on v0

v1 whole, which is shorter than its diff:
```python
import functools

import jax
import jax.numpy as jnp
from jax import lax
from jax.experimental import pallas as pl
from jax.experimental.pallas import tpu as pltpu
from jax.sharding import PartitionSpec as P

STEPS = 4
robin_p = 0.6
MESH = pl.DeviceIdType.MESH
FACE_W = (1.0 - robin_p / 2) / (1.0 + robin_p / 2)
SENT_W = (1.0 - FACE_W) + robin_p * (1.0 + FACE_W) / 2
DATA_W = SENT_W / (1.0 + robin_p / 2)
NB = 4
ROWS = 128
TOP = 8


def places():
    gx, gy = lax.axis_index("gx"), lax.axis_index("gy")
    ngx = lax.axis_size("gx")
    core = gx % 2
    x = ((gx // 2) % 2) * 2 + gy // 4

    def chip(step):
        other = (x + step + 4) % 4
        return ((gx // 4) * 4 + (other // 2) * 2 + core, (other % 2) * 4 + gy % 4)

    def target(of):
        return ((of[0] + 2 * core - 1 + ngx) % ngx, of[1])

    source_gx = (gx - 1 + 2 * core + ngx) % ngx
    source_x = ((source_gx // 2) % 2) * 2 + gy // 4

    def source_relay(step):
        other = (source_x + step + 4) % 4
        return (
            (source_gx // 4) * 4 + (other // 2) * 2 + source_gx % 2,
            (other % 2) * 4 + gy % 4,
        )

    plus, minus = chip(1), chip(-1)
    return dict(
        core=core,
        gy=gy,
        partner=(gx + 1 - 2 * core, gy),
        plus=plus,
        minus=minus,
        target_of_minus=target(minus),
        target_of_plus=target(plus),
        deliver_a=source_relay(1),
        deliver_b=source_relay(-1),
        up=(gx, gy - 1),
        down=(gx, gy + 1),
    )


def kernel(
    init, kap, vel, rat, out,
    u0, u1, u2, u3, v1, v2, v3, o4, kb, vb, rb, ab, got, relay, stage, halo,
    load_sem, out_sem, near_s, near_r, far_s, far_r, hop_s, hop_r, edge_s, edge_r,
):
    here = places()
    core, gy = here["core"], here["gy"]
    last_gy = lax.axis_size("gy") - 1

    loads = []
    for at, (hbm, vmem, top) in enumerate(
        ((init, u0, TOP), (kap, kb, 0), (vel, vb, 0), (rat, rb, 0))
    ):
        for k in range(NB):
            copy = pltpu.make_async_copy(
                hbm.at[:, :, 128 * k : 128 * (k + 1)],
                vmem.at[:, k, top : top + ROWS, :],
                load_sem.at[at * NB + k],
            )
            copy.start()
            loads.append(copy)

    barrier = pltpu.get_barrier_semaphore()
    for who in ("partner", "plus", "minus", "deliver_a", "deliver_b"):
        pl.semaphore_signal(barrier, inc=1, device_id=here[who], device_id_type=MESH)

    @pl.when(gy > 0)
    def _():
        pl.semaphore_signal(barrier, inc=1, device_id=here["up"], device_id_type=MESH)

    @pl.when(gy < last_gy)
    def _():
        pl.semaphore_signal(barrier, inc=1, device_id=here["down"], device_id_type=MESH)

    @pl.when(gy == 0)
    def _():
        for e in range(6):
            halo[e, 0] = jnp.zeros((16, 128), jnp.float32)

    @pl.when(gy == last_gy)
    def _():
        for e in range(6):
            halo[e, 1] = jnp.zeros((16, 128), jnp.float32)

    edges = jnp.where(gy > 0, 1, 0) + jnp.where(gy < last_gy, 1, 0)
    pl.semaphore_wait(barrier, 5 + edges)

    def remote(src, dst, send, recv, who):
        return pltpu.make_async_remote_copy(
            src_ref=src, dst_ref=dst, send_sem=send, recv_sem=recv,
            device_id=here[who], device_id_type=MESH,
        )

    def near_copy(n, ref, top, stride):
        return remote(
            ref.at[(1 - core) * stride, :, top : top + ROWS, :],
            got.at[core, n], near_s.at[n], near_r.at[n], "partner",
        )

    def far_copy(n, ref, top, stride, way):
        return remote(
            ref.at[core * stride, 2 * way : 2 * way + 2, top : top + ROWS, :],
            relay.at[n, way], far_s.at[n, way], hop_r.at[n, way],
            "minus" if way else "plus",
        )

    def hop_copy(n, way):
        return remote(
            relay.at[n, way], got.at[1 - core, n, 2 * way : 2 * way + 2],
            hop_s.at[n, way], far_r.at[n, way],
            "target_of_plus" if way else "target_of_minus",
        )

    sends = []

    def send_faces(n, ref, top, stride):
        for way in range(2):
            copy = far_copy(n, ref, top, stride, way)
            copy.start()
            sends.append(copy)
        copy = near_copy(n, ref, top, stride)
        copy.start()
        sends.append(copy)

    def relay_on(n):
        for way in range(2):
            far_copy(n, u0, TOP, 3, way).wait_recv()
            copy = hop_copy(n, way)
            copy.start()
            sends.append(copy)

    def wait_faces(n):
        near_copy(n, u0, TOP, 3).wait_recv()
        for way in range(2):
            hop_copy(n, way).wait_recv()

    def edge_copies(e):
        up = remote(stage.at[e, 0], halo.at[e, 1], edge_s.at[e, 0], edge_r.at[e, 1], "up")
        down = remote(stage.at[e, 1], halo.at[e, 0], edge_s.at[e, 1], edge_r.at[e, 0], "down")
        return up, down

    def send_edges(e, planes):
        for p, (ref, i) in enumerate(planes):
            for k in range(NB):
                at = p * NB + k
                stage[e, 0, at : at + 1, :] = ref[i, k, TOP : TOP + 1, :]
                stage[e, 1, at : at + 1, :] = ref[i, k, TOP + ROWS - 1 : TOP + ROWS, :]
        up, down = edge_copies(e)

        @pl.when(gy > 0)
        def _():
            up.start()

        @pl.when(gy < last_gy)
        def _():
            down.start()

    def take_edges(e, planes):
        up, down = edge_copies(e)

        @pl.when(gy > 0)
        def _():
            down.wait_recv()

        @pl.when(gy < last_gy)
        def _():
            up.wait_recv()

        for p, (ref, i) in enumerate(planes):
            for k in range(NB):
                at = p * NB + k
                ref[i, k, TOP - 1 : TOP, :] = halo[e, 0, at : at + 1, :]
                ref[i, k, TOP + ROWS : TOP + ROWS + 1, :] = halo[e, 1, at : at + 1, :]

    lane = lax.broadcasted_iota(jnp.int32, (NB, 8, 128), 2)
    at_first, at_last = lane == 0, lane == 127
    zero = jnp.zeros((1, 8, 128), jnp.float32)

    def step(planes, which, dest, dest_top, data=None, fresh=False):
        def body(r, carry):
            row = pl.multiple_of(r * 8, 8)

            def read(p, shift=0):
                ref, i = planes[p]
                return ref[i, :, pl.ds(row + TOP + shift, 8), :]

            need = sorted({q for p in which for q in (p - 1, p, p + 1) if 0 <= q < 4})
            cells = {p: read(p) for p in need}

            def ghost(side, face):
                if data is None:
                    return face * FACE_W
                return face * FACE_W + got[side, data, :, pl.ds(row, 8), :] * DATA_W

            for p in which:
                c = cells[p]
                minus_x = cells[p - 1] if p > 0 else ghost(0, c)
                plus_x = cells[p + 1] if p < 3 else ghost(1, c)
                ahead, behind = pltpu.roll(c, 127, 2), pltpu.roll(c, 1, 2)
                plus_z = jnp.where(at_last, jnp.concatenate([ahead[1:], zero], 0), ahead)
                minus_z = jnp.where(at_first, jnp.concatenate([zero, behind[:-1]], 0), behind)
                total = (plus_x + minus_x) + (read(p, 1) + read(p, -1)) + (plus_z + minus_z)
                k = kb[p, :, pl.ds(row, 8), :]
                v = vb[p, :, pl.ds(row, 8), :]
                q = rb[p, :, pl.ds(row, 8), :]
                if fresh:
                    a = (1.0 - 6.0 * k) - (v + q)
                    ab[p, :, pl.ds(row, 8), :] = a
                else:
                    a = ab[p, :, pl.ds(row, 8), :]
                inner = a + q * pl.reciprocal(1.0 + c * c)
                ref, i = dest[p]
                ref[i, :, pl.ds(row + dest_top, 8), :] = c * inner + (k * total + v * minus_x)
            return carry

        lax.fori_loop(0, ROWS // 8, body, 0)

    def whole(ref):
        return [(ref, p) for p in range(4)]

    a0, a1, a2 = whole(u0), whole(u1), whole(u2)
    a3 = {0: (u3, 0), 3: (u3, 1)}
    b1 = [(v1, 0), (u1, 1), (u1, 2), (v1, 1)]
    b1_edges = [(v1, 0), (v1, 1)]
    b2, b3, b4 = whole(v2), whole(v3), whole(o4)
    outer, inner = (0, 3), (1, 2)

    for copy in loads[:NB]:
        copy.wait()
    send_edges(0, a0)
    send_faces(0, u0, TOP, 3)
    for copy in loads[NB:]:
        copy.wait()
    take_edges(0, a0)
    step(a0, outer, a1, TOP, fresh=True)
    send_faces(1, u1, TOP, 3)
    step(a0, inner, a1, TOP, fresh=True)
    send_edges(1, a1)
    relay_on(0)
    take_edges(1, a1)
    step(a1, outer, a2, TOP)
    send_faces(2, u2, TOP, 3)
    step(a1, inner, a2, TOP)
    send_edges(2, a2)
    take_edges(2, a2)
    step(a2, outer, a3, 0)
    send_faces(3, u3, 0, 1)
    relay_on(1)
    wait_faces(0)
    step(a0, outer, {0: b1[0], 3: b1[3]}, TOP, data=0)
    send_edges(3, b1_edges)
    relay_on(2)
    step(b1, inner, b2, TOP)
    take_edges(3, b1_edges)
    wait_faces(1)
    step(b1, outer, b2, TOP, data=1)
    send_edges(4, b2)
    relay_on(3)
    take_edges(4, b2)
    step(b2, inner, b3, TOP)
    wait_faces(2)
    step(b2, outer, b3, TOP, data=2)
    send_edges(5, b3)
    take_edges(5, b3)
    step(b3, inner, b4, 0)

    def put(first, count, at):
        copies = []
        for k in range(NB):
            copy = pltpu.make_async_copy(
                o4.at[first : first + count, k],
                out.at[first : first + count, :, 128 * k : 128 * (k + 1)],
                out_sem.at[at * NB + k],
            )
            copy.start()
            copies.append(copy)
        return copies

    puts = put(1, 2, 0)
    wait_faces(3)
    step(b3, outer, b4, 0, data=3)
    puts += put(0, 1, 1) + put(3, 1, 2)
    for copy in sends:
        copy.wait_send()
    for e in range(6):
        up, down = edge_copies(e)

        @pl.when(gy > 0)
        def _():
            up.wait_send()

        @pl.when(gy < last_gy)
        def _():
            down.wait_send()

    for copy in puts:
        copy.wait()


def local(initial, kappa, velocity, rate):
    haloed, plain = (4, NB, ROWS + 16, 128), (4, NB, ROWS, 128)
    f32 = lambda *shape: pltpu.VMEM(shape, jnp.float32)
    dma = pltpu.SemaphoreType.DMA
    return pl.pallas_call(
        kernel,
        out_shape=jax.ShapeDtypeStruct(initial.shape, jnp.float32),
        in_specs=[pl.BlockSpec(memory_space=pl.ANY)] * 4,
        out_specs=pl.BlockSpec(memory_space=pl.ANY),
        scratch_shapes=[
            f32(*haloed), f32(*haloed), f32(*haloed), f32(2, NB, ROWS, 128),
            f32(2, NB, ROWS + 16, 128), f32(*haloed), f32(*haloed), f32(*plain),
            f32(*plain), f32(*plain), f32(*plain), f32(*plain),
            f32(2, STEPS, NB, ROWS, 128), f32(STEPS, 2, 2, ROWS, 128),
            f32(6, 2, 16, 128), f32(6, 2, 16, 128),
            dma((16,)), dma((12,)), dma((STEPS,)), dma((STEPS,)),
            dma((STEPS, 2)), dma((STEPS, 2)), dma((STEPS, 2)), dma((STEPS, 2)),
            dma((6, 2)), dma((6, 2)),
        ],
        compiler_params=pltpu.CompilerParams(collective_id=0, has_side_effects=True),
        name="window",
    )(initial, kappa, velocity, rate)


def solution(mesh):
    placed = P("gx", "gy", None)
    return jax.shard_map(
        local, mesh=mesh, in_specs=(placed,) * 4, out_specs=placed, check_vma=False
    )
```

time: 129 us -> 57.7 us (0.45)
  the two profiles are of different devices: /device:TPU:230 before, /device:TPU:24 now
where the time goes in v1:
time: 57.7 us; the launch traced here: 57.5 us
  Pallas kernels  55.3 us (96%)
  local copies, waits for them, and re-layouts  2.26 us (4%)
    pallas_call x1, Pallas kernels, local(): pl.pallas_call(kernel, out_shape=jax.ShapeDtypeStruct(initial.shape, jnp....  55.3 us
    unnamed x1, local copies, waits for them, and re-layouts  2.26 us

profile of v1, /device:TPU:24, one launch (start us, length us, event | category | flops | bytes accessed | tf_op | source)
XLA Modules:
  0.0 57.5 jit_solution(10226669240882835944)
XLA Ops:
  0.0 55.3 %window.1 = f32[4,128,512]{2,1,0:T(8,128)} custom-call(f32[4,128,512]{2,1,0:T(8,128)} %init.1, f32[4,128,512]{2,1,0:T(8,128)} %kap.1, f32[4,128,512]{2,1,0:T(8,128)} %vel.1, f32[4,128,512]{2,1,0:T(8,128)} %rat.1), custom_call_target="tpu_custom_call" | custom-call | tf_op jit(solution)/shard_map/window/pallas_call | solution.py:323
  55.3 2.3 %copy.6 = f32[4,128,512]{2,1,0:T(8,128)} copy(f32[4,128,512]{2,1,0:T(8,128)} %window.1) | data formatting | bytes 2097152

commit v2 on v1

v2 whole, which is shorter than its diff:
```python
import jax
import jax.numpy as jnp
from jax import lax
from jax.experimental import pallas as pl
from jax.experimental.pallas import tpu as pltpu
from jax.sharding import PartitionSpec as P

STEPS = 4
robin_p = 0.6
MESH = pl.DeviceIdType.MESH
FACE_W = (1.0 - robin_p / 2) / (1.0 + robin_p / 2)
SENT_W = (1.0 - FACE_W) + robin_p * (1.0 + FACE_W) / 2
DATA_W = SENT_W / (1.0 + robin_p / 2)
NB = 4
ROWS = 128
TOP = 8
MARGIN = 4


def places():
    gx, gy = lax.axis_index("gx"), lax.axis_index("gy")
    ngx = lax.axis_size("gx")
    core = gx % 2
    x = ((gx // 2) % 2) * 2 + gy // 4

    def chip(step):
        other = (x + step + 4) % 4
        return ((gx // 4) * 4 + (other // 2) * 2 + core, (other % 2) * 4 + gy % 4)

    def target(of):
        return ((of[0] + 2 * core - 1 + ngx) % ngx, of[1])

    source_gx = (gx - 1 + 2 * core + ngx) % ngx
    source_x = ((source_gx // 2) % 2) * 2 + gy // 4

    def source_relay(step):
        other = (source_x + step + 4) % 4
        return (
            (source_gx // 4) * 4 + (other // 2) * 2 + source_gx % 2,
            (other % 2) * 4 + gy % 4,
        )

    plus, minus = chip(1), chip(-1)
    return dict(
        core=core,
        gy=gy,
        partner=(gx + 1 - 2 * core, gy),
        plus=plus,
        minus=minus,
        target_of_minus=target(minus),
        target_of_plus=target(plus),
        deliver_a=source_relay(1),
        deliver_b=source_relay(-1),
        up=(gx, gy - 1),
        down=(gx, gy + 1),
    )


def kernel(
    init, kap, vel, rat, out,
    u0, u1, u2, u3, v1, v2, v3, o4, kb, vb, rb, ab, got, relay,
    load_sem, out_sem, near_s, near_r, far_s, far_r, hop_s, hop_r, edge_s, edge_r,
):
    here = places()
    core, gy = here["core"], here["gy"]
    last_gy = lax.axis_size("gy") - 1
    arrays = ((init, u0), (kap, kb), (vel, vb), (rat, rb))

    loads = []
    for at, (hbm, vmem) in enumerate(arrays):
        for k in range(NB):
            copy = pltpu.make_async_copy(
                hbm.at[:, :, 128 * k : 128 * (k + 1)],
                vmem.at[:, k, TOP : TOP + ROWS, :],
                load_sem.at[at * NB + k],
            )
            copy.start()
            loads.append(copy)

    barrier = pltpu.get_barrier_semaphore()
    for who in ("partner", "plus", "minus", "deliver_a", "deliver_b"):
        pl.semaphore_signal(barrier, inc=1, device_id=here[who], device_id_type=MESH)

    @pl.when(gy > 0)
    def _():
        pl.semaphore_signal(barrier, inc=1, device_id=here["up"], device_id_type=MESH)

    @pl.when(gy < last_gy)
    def _():
        pl.semaphore_signal(barrier, inc=1, device_id=here["down"], device_id_type=MESH)

    @pl.when(gy == 0)
    def _():
        for _, vmem in arrays:
            vmem[:, :, 0:TOP, :] = jnp.zeros((4, NB, TOP, 128), jnp.float32)

    @pl.when(gy == last_gy)
    def _():
        for _, vmem in arrays:
            vmem[:, :, TOP + ROWS :, :] = jnp.zeros((4, NB, TOP, 128), jnp.float32)

    edges = jnp.where(gy > 0, 1, 0) + jnp.where(gy < last_gy, 1, 0)
    pl.semaphore_wait(barrier, 5 + edges)

    def remote(src, dst, send, recv, who):
        return pltpu.make_async_remote_copy(
            src_ref=src, dst_ref=dst, send_sem=send, recv_sem=recv,
            device_id=here[who], device_id_type=MESH,
        )

    def edge_copies(down):
        for at, (hbm, vmem) in enumerate(arrays):
            for k in range(NB):
                i = at * NB + k
                taken = ROWS - MARGIN if down else 0
                put = TOP - MARGIN if down else TOP + ROWS
                yield remote(
                    hbm.at[:, taken : taken + MARGIN, 128 * k : 128 * (k + 1)],
                    vmem.at[:, k, put : put + MARGIN, :],
                    edge_s.at[down, i], edge_r.at[down, i], "down" if down else "up",
                )

    @pl.when(gy > 0)
    def _():
        for copy in edge_copies(0):
            copy.start()

    @pl.when(gy < last_gy)
    def _():
        for copy in edge_copies(1):
            copy.start()

    def take_edges():
        @pl.when(gy > 0)
        def _():
            for copy in edge_copies(1):
                copy.wait_recv()

        @pl.when(gy < last_gy)
        def _():
            for copy in edge_copies(0):
                copy.wait_recv()

    pieces = (
        (0, TOP, ROWS),
        (0, TOP - MARGIN, MARGIN),
        (0, TOP + ROWS, MARGIN),
        (1, TOP - 2, ROWS + 4),
        (2, TOP - 1, ROWS + 2),
        (3, TOP, ROWS),
    )

    def near_copy(j, ref, stride):
        n, row, rows = pieces[j]
        return remote(
            ref.at[(1 - core) * stride, :, row : row + rows, :],
            got.at[core, n, :, row : row + rows, :], near_s.at[j], near_r.at[j], "partner",
        )

    def far_copy(j, ref, stride, way):
        n, row, rows = pieces[j]
        return remote(
            ref.at[core * stride, 2 * way : 2 * way + 2, row : row + rows, :],
            relay.at[n, way, :, row : row + rows, :], far_s.at[j, way], hop_r.at[j, way],
            "minus" if way else "plus",
        )

    def hop_copy(j, way):
        n, row, rows = pieces[j]
        return remote(
            relay.at[n, way, :, row : row + rows, :],
            got.at[1 - core, n, 2 * way : 2 * way + 2, row : row + rows, :],
            hop_s.at[j, way], far_r.at[j, way],
            "target_of_plus" if way else "target_of_minus",
        )

    sends = []

    def go(copy):
        copy.start()
        sends.append(copy)

    def send_faces(j, ref, stride):
        for way in range(2):
            go(far_copy(j, ref, stride, way))
        go(near_copy(j, ref, stride))

    def relay_on(j):
        for way in range(2):
            far_copy(j, u0, 3, way).wait_recv()
            go(hop_copy(j, way))

    def wait_faces(j):
        near_copy(j, u0, 3).wait_recv()
        for way in range(2):
            hop_copy(j, way).wait_recv()

    lane = lax.broadcasted_iota(jnp.int32, (NB, 8, 128), 2)
    at_first, at_last = lane == 0, lane == 127
    zero = jnp.zeros((1, 8, 128), jnp.float32)

    def step(planes, which, dest, tiles, first, data=None, fresh=False, drop=0):
        def tile(row):
            here_rows = pl.ds(row, 8)

            def read(p, shift=0):
                ref, i = planes[p]
                return ref[i, :, pl.ds(row + shift, 8), :]

            need = sorted({q for p in which for q in (p - 1, p, p + 1) if 0 <= q < 4})
            cells = {p: read(p) for p in need}

            def ghost(side, face):
                if data is None:
                    return face * FACE_W
                return face * FACE_W + got[side, data, :, here_rows, :] * DATA_W

            results = []
            for p in which:
                c = cells[p]
                minus_x = cells[p - 1] if p > 0 else ghost(0, c)
                plus_x = cells[p + 1] if p < 3 else ghost(1, c)
                ahead, behind = pltpu.roll(c, 127, 2), pltpu.roll(c, 1, 2)
                plus_z = jnp.where(at_last, jnp.concatenate([ahead[1:], zero], 0), ahead)
                minus_z = jnp.where(at_first, jnp.concatenate([zero, behind[:-1]], 0), behind)
                total = (plus_x + minus_x) + (read(p, 1) + read(p, -1)) + (plus_z + minus_z)
                k = kb[p, :, here_rows, :]
                v = vb[p, :, here_rows, :]
                q = rb[p, :, here_rows, :]
                a = (1.0 - 6.0 * k) - (v + q) if fresh else ab[p, :, here_rows, :]
                inner = a + q * pl.reciprocal(1.0 + c * c)
                results.append((p, a, c * inner + (k * total + v * minus_x)))
            return results

        def store(row, results):
            for p, a, value in results:
                if fresh:
                    ab[p, :, pl.ds(row, 8), :] = a
                ref, i = dest[p]
                ref[i, :, pl.ds(row - drop, 8), :] = value

        begin, end = tiles
        pairs = (end - begin) // 2

        def body(t, carry):
            row = pl.multiple_of(t * 16, 16) + (first + 8 * begin)
            one, two = tile(row), tile(row + 8)
            store(row, one)
            store(row + 8, two)
            return carry

        if pairs > 1:
            lax.fori_loop(0, pairs, body, 0)
        elif pairs:
            body(0, 0)
        if (end - begin) % 2:
            row = first + 8 * (end - 1)
            store(row, tile(row))

    def whole(ref):
        return [(ref, p) for p in range(4)]

    a0, a1, a2 = whole(u0), whole(u1), whole(u2)
    a3 = {0: (u3, 0), 3: (u3, 1)}
    b1 = [(v1, 0), (u1, 1), (u1, 2), (v1, 1)]
    b2, b3, b4 = whole(v2), whole(v3), whole(o4)
    outer, inner = (0, 3), (1, 2)
    wide = ((0, 17), TOP - MARGIN)
    plain = ((0, 16), TOP)

    for copy in loads[:NB]:
        copy.wait()
    send_faces(0, u0, 3)
    for copy in loads[NB:]:
        copy.wait()
    for which in (outer, inner):
        step(a0, which, a1, (1, 15), TOP - MARGIN, fresh=True)
    take_edges()
    send_faces(1, u0, 3)
    send_faces(2, u0, 3)
    for tiles in ((0, 1), (15, 17)):
        step(a0, outer, a1, tiles, TOP - MARGIN, fresh=True)
    send_faces(3, u1, 3)
    for tiles in ((0, 1), (15, 17)):
        step(a0, inner, a1, tiles, TOP - MARGIN, fresh=True)
    relay_on(0)
    step(a1, outer, a2, *wide)
    send_faces(4, u2, 3)
    step(a1, inner, a2, *wide)
    step(a2, outer, a3, *plain)
    send_faces(5, u3, 1)
    for j in (1, 2, 3):
        relay_on(j)
    for j in (0, 1, 2):
        wait_faces(j)
    step(a0, outer, {0: b1[0], 3: b1[3]}, *wide, data=0)
    relay_on(4)
    step(b1, inner, b2, *wide)
    relay_on(5)
    wait_faces(3)
    step(b1, outer, b2, *wide, data=1)
    step(b2, inner, b3, *wide)
    wait_faces(4)
    step(b2, outer, b3, *wide, data=2)
    step(b3, inner, b4, *plain, drop=TOP)

    def put(first, count, at):
        copies = []
        for k in range(NB):
            copy = pltpu.make_async_copy(
                o4.at[first : first + count, k],
                out.at[first : first + count, :, 128 * k : 128 * (k + 1)],
                out_sem.at[at * NB + k],
            )
            copy.start()
            copies.append(copy)
        return copies

    puts = put(1, 2, 0)
    wait_faces(5)
    step(b3, outer, b4, *plain, data=3, drop=TOP)
    puts += put(0, 1, 1) + put(3, 1, 2)
    for copy in sends:
        copy.wait_send()

    @pl.when(gy > 0)
    def _():
        for copy in edge_copies(0):
            copy.wait_send()

    @pl.when(gy < last_gy)
    def _():
        for copy in edge_copies(1):
            copy.wait_send()

    for copy in puts:
        copy.wait()


def local(initial, kappa, velocity, rate):
    tall = ROWS + 2 * TOP
    f32 = lambda *shape: pltpu.VMEM(shape, jnp.float32)
    full, pair = f32(4, NB, tall, 128), f32(2, NB, tall, 128)
    dma = pltpu.SemaphoreType.DMA
    return pl.pallas_call(
        kernel,
        out_shape=jax.ShapeDtypeStruct(initial.shape, jnp.float32),
        in_specs=[pl.BlockSpec(memory_space=pl.ANY)] * 4,
        out_specs=pl.BlockSpec(memory_space=pl.ANY),
        scratch_shapes=[
            full, full, full, pair, pair, full, full, f32(4, NB, ROWS, 128),
            full, full, full, full,
            f32(2, STEPS, NB, tall, 128), f32(STEPS, 2, 2, tall, 128),
            dma((16,)), dma((12,)), dma((6,)), dma((6,)),
            dma((6, 2)), dma((6, 2)), dma((6, 2)), dma((6, 2)),
            dma((2, 16)), dma((2, 16)),
        ],
        compiler_params=pltpu.CompilerParams(collective_id=0, has_side_effects=True),
        name="window",
    )(initial, kappa, velocity, rate)


def solution(mesh):
    placed = P("gx", "gy", None)
    return jax.shard_map(
        local, mesh=mesh, in_specs=(placed,) * 4, out_specs=placed, check_vma=False
    )
```

time: 57.7 us -> 48.5 us (0.84)
  the two profiles are of different devices: /device:TPU:24 before, /device:TPU:2 now
where the time goes in v2:
time: 48.5 us; the launch traced here: 48.4 us
  Pallas kernels  46.1 us (95%)
  local copies, waits for them, and re-layouts  2.26 us (5%)
    pallas_call x1, Pallas kernels, local(): pl.pallas_call(kernel, out_shape=jax.ShapeDtypeStruct(initial.shape, jnp....  46.1 us
    unnamed x1, local copies, waits for them, and re-layouts  2.26 us

profile of v2, /device:TPU:2, one launch (start us, length us, event | category | flops | bytes accessed | tf_op | source)
XLA Modules:
  0.0 48.4 jit_solution(16988799469129635872)
XLA Ops:
  0.0 46.1 %window.1 = f32[4,128,512]{2,1,0:T(8,128)} custom-call(f32[4,128,512]{2,1,0:T(8,128)} %init.1, f32[4,128,512]{2,1,0:T(8,128)} %kap.1, f32[4,128,512]{2,1,0:T(8,128)} %vel.1, f32[4,128,512]{2,1,0:T(8,128)} %rat.1), custom_call_target="tpu_custom_call" | custom-call | tf_op jit(solution)/shard_map/window/pallas_call | solution.py:345
  46.1 2.3 %copy.6 = f32[4,128,512]{2,1,0:T(8,128)} copy(f32[4,128,512]{2,1,0:T(8,128)} %window.1) | data formatting | bytes 2097152

commit v3 on v2

--- a/solution.py
+++ b/solution.py
@@ -58,8 +58,8 @@
 
 def kernel(
     init, kap, vel, rat, out,
-    u0, u1, u2, u3, v1, v2, v3, o4, kb, vb, rb, ab, got, relay,
-    load_sem, out_sem, near_s, near_r, far_s, far_r, hop_s, hop_r, edge_s, edge_r,
+    u0, u1, u2, u3, v1, v2, v3, kb, vb, rb, ab, got, relay,
+    load_sem, near_s, near_r, far_s, far_r, hop_s, hop_r, edge_s, edge_r,
 ):
     here = places()
     core, gy = here["core"], here["gy"]
@@ -108,17 +108,84 @@
             device_id=here[who], device_id_type=MESH,
         )
 
+    pieces = (
+        (0, TOP, ROWS, 0, 1),
+        (0, TOP, ROWS, 1, 1),
+        (0, TOP - MARGIN, MARGIN, 0, 2),
+        (0, TOP + ROWS, MARGIN, 0, 2),
+        (1, TOP - 2, ROWS + 4, 0, 2),
+        (2, TOP - 1, ROWS + 2, 0, 2),
+        (3, TOP, ROWS, 0, 1),
+        (3, TOP, ROWS, 1, 1),
+    )
+
+    def near_copy(n, ref, stride):
+        row = (TOP - MARGIN, TOP - 2, TOP - 1, TOP)[n]
+        rows = ROWS + 2 * (TOP - row)
+        return remote(
+            ref.at[(1 - core) * stride, :, row : row + rows, :],
+            got.at[core, n, :, row : row + rows, :], near_s.at[n], near_r.at[n], "partner",
+        )
+
+    def far_copy(j, ref, stride, way):
+        n, row, rows, k, blocks = pieces[j]
+        if ref is init:
+            lanes = slice(128 * (2 * way + k), 128 * (2 * way + k + 1))
+            src, dst = ref.at[core * stride, :, lanes], relay.at[n, way, k, row : row + rows, :]
+        else:
+            src = ref.at[core * stride, 2 * way + k : 2 * way + k + blocks, row : row + rows, :]
+            dst = relay.at[n, way, k : k + blocks, row : row + rows, :]
+        return remote(
+            src, dst, far_s.at[j, way], hop_r.at[j, way], "minus" if way else "plus"
+        )
+
+    def hop_copy(j, way):
+        n, row, rows, k, blocks = pieces[j]
+        return remote(
+            relay.at[n, way, k : k + blocks, row : row + rows, :],
+            got.at[1 - core, n, 2 * way + k : 2 * way + k + blocks, row : row + rows, :],
+            hop_s.at[j, way], far_r.at[j, way],
+            "target_of_plus" if way else "target_of_minus",
+        )
+
+    sends = []
+
+    def go(copy):
+        copy.start()
+        sends.append(copy)
+
+    def send_far(js, ref, stride):
+        for j in js:
+            for way in range(2):
+                go(far_copy(j, ref, stride, way))
+
+    def relay_on(js):
+        for j in js:
+            for way in range(2):
+                far_copy(j, u0, 3, way).wait_recv()
+                go(hop_copy(j, way))
+
+    def wait_faces(n):
+        near_copy(n, u0, 3).wait_recv()
+        for j in range(len(pieces)):
+            if pieces[j][0] == n:
+                for way in range(2):
+                    hop_copy(j, way).wait_recv()
+
+    send_far((0, 1), init, 3)
+
     def edge_copies(down):
-        for at, (hbm, vmem) in enumerate(arrays):
-            for k in range(NB):
-                i = at * NB + k
-                taken = ROWS - MARGIN if down else 0
-                put = TOP - MARGIN if down else TOP + ROWS
-                yield remote(
-                    hbm.at[:, taken : taken + MARGIN, 128 * k : 128 * (k + 1)],
-                    vmem.at[:, k, put : put + MARGIN, :],
-                    edge_s.at[down, i], edge_r.at[down, i], "down" if down else "up",
-                )
+        for i, (_, vmem) in enumerate(arrays):
+            rows = MARGIN if i == 0 else MARGIN - 1
+            taken = TOP + ROWS - rows if down else TOP
+            put = TOP - rows if down else TOP + ROWS
+            yield remote(
+                vmem.at[:, :, taken : taken + rows, :], vmem.at[:, :, put : put + rows, :],
+                edge_s.at[down, i], edge_r.at[down, i], "down" if down else "up",
+            )
+
+    for copy in loads:
+        copy.wait()
 
     @pl.when(gy > 0)
     def _():
@@ -141,65 +208,11 @@
             for copy in edge_copies(0):
                 copy.wait_recv()
 
-    pieces = (
-        (0, TOP, ROWS),
-        (0, TOP - MARGIN, MARGIN),
-        (0, TOP + ROWS, MARGIN),
-        (1, TOP - 2, ROWS + 4),
-        (2, TOP - 1, ROWS + 2),
-        (3, TOP, ROWS),
-    )
-
-    def near_copy(j, ref, stride):
-        n, row, rows = pieces[j]
-        return remote(
-            ref.at[(1 - core) * stride, :, row : row + rows, :],
-            got.at[core, n, :, row : row + rows, :], near_s.at[j], near_r.at[j], "partner",
-        )
-
-    def far_copy(j, ref, stride, way):
-        n, row, rows = pieces[j]
-        return remote(
-            ref.at[core * stride, 2 * way : 2 * way + 2, row : row + rows, :],
-            relay.at[n, way, :, row : row + rows, :], far_s.at[j, way], hop_r.at[j, way],
-            "minus" if way else "plus",
-        )
-
-    def hop_copy(j, way):
-        n, row, rows = pieces[j]
-        return remote(
-            relay.at[n, way, :, row : row + rows, :],
-            got.at[1 - core, n, 2 * way : 2 * way + 2, row : row + rows, :],
-            hop_s.at[j, way], far_r.at[j, way],
-            "target_of_plus" if way else "target_of_minus",
-        )
-
-    sends = []
-
-    def go(copy):
-        copy.start()
-        sends.append(copy)
-
-    def send_faces(j, ref, stride):
-        for way in range(2):
-            go(far_copy(j, ref, stride, way))
-        go(near_copy(j, ref, stride))
-
-    def relay_on(j):
-        for way in range(2):
-            far_copy(j, u0, 3, way).wait_recv()
-            go(hop_copy(j, way))
-
-    def wait_faces(j):
-        near_copy(j, u0, 3).wait_recv()
-        for way in range(2):
-            hop_copy(j, way).wait_recv()
-
     lane = lax.broadcasted_iota(jnp.int32, (NB, 8, 128), 2)
     at_first, at_last = lane == 0, lane == 127
     zero = jnp.zeros((1, 8, 128), jnp.float32)
 
-    def step(planes, which, dest, tiles, first, data=None, fresh=False, drop=0):
+    def step(planes, which, dest, tiles, first, data=None, fresh=False):
         def tile(row):
             here_rows = pl.ds(row, 8)
 
@@ -236,8 +249,12 @@
             for p, a, value in results:
                 if fresh:
                     ab[p, :, pl.ds(row, 8), :] = a
-                ref, i = dest[p]
-                ref[i, :, pl.ds(row - drop, 8), :] = value
+                if dest is None:
+                    for k in range(NB):
+                        out[p, pl.ds(row - TOP, 8), 128 * k : 128 * (k + 1)] = value[k]
+                else:
+                    ref, i = dest[p]
+                    ref[i, :, pl.ds(row, 8), :] = value
 
         begin, end = tiles
         pairs = (end - begin) // 2
@@ -263,63 +280,44 @@
     a0, a1, a2 = whole(u0), whole(u1), whole(u2)
     a3 = {0: (u3, 0), 3: (u3, 1)}
     b1 = [(v1, 0), (u1, 1), (u1, 2), (v1, 1)]
-    b2, b3, b4 = whole(v2), whole(v3), whole(o4)
+    b2, b3 = whole(v2), whole(v3)
     outer, inner = (0, 3), (1, 2)
     wide = ((0, 17), TOP - MARGIN)
     plain = ((0, 16), TOP)
 
-    for copy in loads[:NB]:
-        copy.wait()
-    send_faces(0, u0, 3)
-    for copy in loads[NB:]:
-        copy.wait()
     for which in (outer, inner):
         step(a0, which, a1, (1, 15), TOP - MARGIN, fresh=True)
+    relay_on((0, 1))
     take_edges()
-    send_faces(1, u0, 3)
-    send_faces(2, u0, 3)
     for tiles in ((0, 1), (15, 17)):
         step(a0, outer, a1, tiles, TOP - MARGIN, fresh=True)
-    send_faces(3, u1, 3)
+    send_far((4,), u1, 3)
+    send_far((2, 3), u0, 3)
+    go(near_copy(0, u0, 3))
+    go(near_copy(1, u1, 3))
     for tiles in ((0, 1), (15, 17)):
         step(a0, inner, a1, tiles, TOP - MARGIN, fresh=True)
-    relay_on(0)
     step(a1, outer, a2, *wide)
-    send_faces(4, u2, 3)
+    send_far((5,), u2, 3)
+    go(near_copy(2, u2, 3))
     step(a1, inner, a2, *wide)
     step(a2, outer, a3, *plain)
-    send_faces(5, u3, 1)
-    for j in (1, 2, 3):
-        relay_on(j)
-    for j in (0, 1, 2):
-        wait_faces(j)
+    send_far((6, 7), u3, 1)
+    go(near_copy(3, u3, 1))
+    relay_on((4, 2, 3))
+    wait_faces(0)
     step(a0, outer, {0: b1[0], 3: b1[3]}, *wide, data=0)
-    relay_on(4)
+    relay_on((5,))
     step(b1, inner, b2, *wide)
-    relay_on(5)
-    wait_faces(3)
+    relay_on((6, 7))
+    wait_faces(1)
     step(b1, outer, b2, *wide, data=1)
     step(b2, inner, b3, *wide)
-    wait_faces(4)
+    wait_faces(2)
     step(b2, outer, b3, *wide, data=2)
-    step(b3, inner, b4, *plain, drop=TOP)
-
-    def put(first, count, at):
-        copies = []
-        for k in range(NB):
-            copy = pltpu.make_async_copy(
-                o4.at[first : first + count, k],
-                out.at[first : first + count, :, 128 * k : 128 * (k + 1)],
-                out_sem.at[at * NB + k],
-            )
-            copy.start()
-            copies.append(copy)
-        return copies
-
-    puts = put(1, 2, 0)
-    wait_faces(5)
-    step(b3, outer, b4, *plain, data=3, drop=TOP)
-    puts += put(0, 1, 1) + put(3, 1, 2)
+    step(b3, inner, None, *plain)
+    wait_faces(3)
+    step(b3, outer, None, *plain, data=3)
     for copy in sends:
         copy.wait_send()
 
@@ -332,9 +330,6 @@
     def _():
         for copy in edge_copies(1):
             copy.wait_send()
-
-    for copy in puts:
-        copy.wait()
 
 
 def local(initial, kappa, velocity, rate):
@@ -345,19 +340,21 @@
     return pl.pallas_call(
         kernel,
         out_shape=jax.ShapeDtypeStruct(initial.shape, jnp.float32),
-        in_specs=[pl.BlockSpec(memory_space=pl.ANY)] * 4,
-        out_specs=pl.BlockSpec(memory_space=pl.ANY),
+        in_specs=[pl.BlockSpec(memory_space=pltpu.HBM)] * 4,
+        out_specs=pl.BlockSpec(memory_space=pltpu.VMEM),
         scratch_shapes=[
-            full, full, full, pair, pair, full, full, f32(4, NB, ROWS, 128),
+            full, full, full, pair, pair, full, full,
             full, full, full, full,
             f32(2, STEPS, NB, tall, 128), f32(STEPS, 2, 2, tall, 128),
-            dma((16,)), dma((12,)), dma((6,)), dma((6,)),
-            dma((6, 2)), dma((6, 2)), dma((6, 2)), dma((6, 2)),
-            dma((2, 16)), dma((2, 16)),
+            dma((16,)), dma((STEPS,)), dma((STEPS,)),
+            dma((8, 2)), dma((8, 2)), dma((8, 2)), dma((8, 2)),
+            dma((2, 4)), dma((2, 4)),
         ],
-        compiler_params=pltpu.CompilerParams(collective_id=0, has_side_effects=True),
+        compiler_params=pltpu.CompilerParams(
+            collective_id=0, has_side_effects=True, vmem_limit_bytes=40 * 2**20
+        ),
         name="window",
-    )(initial, kappa, velocity, rate)
+    )(*(pltpu.with_memory_space_constraint(x, pltpu.HBM) for x in (initial, kappa, velocity, rate)))
 
 
 def solution(mesh):

time: 48.5 us -> 46.3 us (0.955)
  the two profiles are of different devices: /device:TPU:2 before, /device:TPU:26 now
where the time goes in v3:
time: 46.3 us; the launch traced here: 46.1 us
  Pallas kernels  45.2 us (98%)
  local copies, waits for them, and re-layouts  0.97 us (2%)
    pallas_call x1, Pallas kernels, local(): pl.pallas_call(kernel, out_shape=jax.ShapeDtypeStruct(initial.shape, jnp....  45.2 us
    unnamed x1, local copies, waits for them, and re-layouts  0.97 us

profile of v3, /device:TPU:26, one launch (start us, length us, event | category | flops | bytes accessed | tf_op | source)
XLA Modules:
  0.0 46.1 jit_solution(13621639427021308198)
XLA Ops:
  0.0 45.2 %window.1 = f32[4,128,512]{2,1,0:T(8,128)S(1)} custom-call(f32[4,128,512]{2,1,0:T(8,128)} %init.1, f32[4,128,512]{2,1,0:T(8,128)} %kap.1, f32[4,128,512]{2,1,0:T(8,128)} %vel.1, f32[4,128,512]{2,1,0:T(8,128)} %rat.1), custom_call_target="tpu_custom_call" | custom-call | tf_op jit(solution)/shard_map/window/pallas_call | solution.py:340
  45.2 1.0 %copy.6 = f32[4,128,512]{2,1,0:T(8,128)} copy(f32[4,128,512]{2,1,0:T(8,128)S(1)} %window.1) | data formatting | bytes 2097152

commit v4 on v3

--- a/solution.py
+++ b/solution.py
@@ -172,8 +172,6 @@
                 for way in range(2):
                     hop_copy(j, way).wait_recv()
 
-    send_far((0, 1), init, 3)
-
     def edge_copies(down):
         for i, (_, vmem) in enumerate(arrays):
             rows = MARGIN if i == 0 else MARGIN - 1
@@ -207,6 +205,8 @@
         def _():
             for copy in edge_copies(0):
                 copy.wait_recv()
+
+    send_far((0, 1), u0, 3)
 
     lane = lax.broadcasted_iota(jnp.int32, (NB, 8, 128), 2)
     at_first, at_last = lane == 0, lane == 127
@@ -302,9 +302,9 @@
     go(near_copy(2, u2, 3))
     step(a1, inner, a2, *wide)
     step(a2, outer, a3, *plain)
+    relay_on((4, 2, 3))
     send_far((6, 7), u3, 1)
     go(near_copy(3, u3, 1))
-    relay_on((4, 2, 3))
     wait_faces(0)
     step(a0, outer, {0: b1[0], 3: b1[3]}, *wide, data=0)
     relay_on((5,))

time: 46.3 us -> 43.2 us (0.933)
  the two profiles are of different devices: /device:TPU:26 before, /device:TPU:2 now
where the time goes in v4:
time: 43.2 us; the launch traced here: 43.1 us
  Pallas kernels  42.1 us (97%)
  local copies, waits for them, and re-layouts  0.97 us (2%)
    pallas_call x1, Pallas kernels, local(): pl.pallas_call(kernel, out_shape=jax.ShapeDtypeStruct(initial.shape, jnp....  42.1 us
    unnamed x1, local copies, waits for them, and re-layouts  0.97 us

profile of v4, /device:TPU:2, one launch (start us, length us, event | category | flops | bytes accessed | tf_op | source)
XLA Modules:
  0.0 43.1 jit_solution(9838190565350386422)
XLA Ops:
  0.0 42.1 %window.1 = f32[4,128,512]{2,1,0:T(8,128)S(1)} custom-call(f32[4,128,512]{2,1,0:T(8,128)} %init.1, f32[4,128,512]{2,1,0:T(8,128)} %kap.1, f32[4,128,512]{2,1,0:T(8,128)} %vel.1, f32[4,128,512]{2,1,0:T(8,128)} %rat.1), custom_call_target="tpu_custom_call" | custom-call | tf_op jit(solution)/shard_map/window/pallas_call | solution.py:340
  42.1 1.0 %copy.6 = f32[4,128,512]{2,1,0:T(8,128)} copy(f32[4,128,512]{2,1,0:T(8,128)S(1)} %window.1) | data formatting | bytes 2097152

commit v5 on v4

--- a/solution.py
+++ b/solution.py
@@ -302,9 +302,10 @@
     go(near_copy(2, u2, 3))
     step(a1, inner, a2, *wide)
     step(a2, outer, a3, *plain)
-    relay_on((4, 2, 3))
+    relay_on((4,))
     send_far((6, 7), u3, 1)
     go(near_copy(3, u3, 1))
+    relay_on((2, 3))
     wait_faces(0)
     step(a0, outer, {0: b1[0], 3: b1[3]}, *wide, data=0)
     relay_on((5,))

time: 43.2 us -> 44.5 us (1.030)
  the two profiles are of different devices: /device:TPU:2 before, /device:TPU:26 now
where the time goes in v5:
time: 44.5 us; the launch traced here: 44.4 us
  Pallas kernels  43.4 us (98%)
  local copies, waits for them, and re-layouts  0.97 us (2%)
    pallas_call x1, Pallas kernels, local(): pl.pallas_call(kernel, out_shape=jax.ShapeDtypeStruct(initial.shape, jnp....  43.4 us
    unnamed x1, local copies, waits for them, and re-layouts  0.97 us

profile of v5, /device:TPU:26, one launch (start us, length us, event | category | flops | bytes accessed | tf_op | source)
XLA Modules:
  0.0 44.4 jit_solution(544566058308605347)
XLA Ops:
  0.0 43.4 %window.1 = f32[4,128,512]{2,1,0:T(8,128)S(1)} custom-call(f32[4,128,512]{2,1,0:T(8,128)} %init.1, f32[4,128,512]{2,1,0:T(8,128)} %kap.1, f32[4,128,512]{2,1,0:T(8,128)} %vel.1, f32[4,128,512]{2,1,0:T(8,128)} %rat.1), custom_call_target="tpu_custom_call" | custom-call | tf_op jit(solution)/shard_map/window/pallas_call | solution.py:341
  43.4 1.0 %copy.6 = f32[4,128,512]{2,1,0:T(8,128)} copy(f32[4,128,512]{2,1,0:T(8,128)S(1)} %window.1) | data formatting | bytes 2097152
